TPU v7x, 256 devices: a whole 4x4x8 slice. The times are simulated.
256 devices in a mesh: tok: 64 (over z, y, core), rep: 4 (over x).
Axes of the slice: x: 4, y: 4, z: 8, core: 2. Of those that a mesh axis runs over, the one named last changes fastest.
Arguments:
- patches: bfloat16 [65536, 768], P(('tok', 'rep')), may hold values from -6 to 6
- patch_view: int32 [65536], P(('tok', 'rep')), may hold values from 0 to 511
- rays: bfloat16 [65536, 768], P(('tok', 'rep')), may hold values from -24 to 24
- ray_view: int32 [65536], P(('tok', 'rep')), may hold values from 0 to 511
- targets: float32 [3, 65536], P(None, ('tok', 'rep')), may hold values from -6 to 6
- camera: bfloat16 [512, 768], P('tok'), may hold values from -6 to 6
- slots_init: float32 [64, 768], replicated, may hold values from -6 to 6
- key_weight: bfloat16 [768, 768], P('tok'), may hold values from -0.875 to 0.875
- value_weight: bfloat16 [768, 768], P('tok'), may hold values from -0.4375 to 0.4375
- query_weight: bfloat16 [768, 768], P('tok'), may hold values from -0.21875 to 0.21875
- gru_input: bfloat16 [768, 2304], P('tok'), may hold values from -0.21875 to 0.21875
- gru_hidden: bfloat16 [768, 2304], P('tok'), may hold values from -0.21875 to 0.21875
- mix_query: bfloat16 [768, 768], P('tok'), may hold values from -0.875 to 0.875
- mix_key: bfloat16 [768, 768], P('tok'), may hold values from -0.21875 to 0.21875
- render_in: bfloat16 [768, 1536], P('tok'), may hold values from -0.21875 to 0.21875
- render_out: bfloat16 [3, 1536], P(None, 'tok'), may hold values from -0.15625 to 0.15625
Outputs:
- slots_out: float32 [64, 768], replicated
- colour: float32 [3, 65536], P(None, ('tok', 'rep'))
- loss: float32 [], replicated
- grad_render_in: float32 [768, 1536], P('tok')
- grad_render_out: float32 [3, 1536], replicated
All inputs are finite; a program needn't handle non-finite values.
Results may differ from a plain program's by a relative error of at most 0.019.
Values may be sent and summed in bfloat16 or wider, within the bound.
A program may use at most 128 MiB of HBM per device.

v0:
```python
import jax
import jax.numpy as jnp
from jax import lax
from jax.sharding import Mesh
from jax.sharding import PartitionSpec as P

ITERS = 3
TOK = ("tok_0", "tok_1", "tok_2")
TOK_REP = ("tok_0", "tok_1", "tok_2", "rep")
EPSILON = 1e-05
ATTN_FLOOR = 1e-08


def from_everyone(value, axis):
    size = lax.axis_size(axis)
    return lax.all_to_all(
        jnp.broadcast_to(value[None], (size, *value.shape)), axis, 0, 0, tiled=True
    )


def in_order(parts, dim):
    parts = jnp.moveaxis(parts, 0, dim)
    lengths = parts.shape
    return parts.reshape(*lengths[:dim], lengths[dim] * lengths[dim + 1], *lengths[dim + 2 :])


def gathered_copies(value, axis, dim):
    parts = from_everyone(value, axis)
    return in_order(parts, dim)


def in_one_piece(arrays, axis, dim, along):
    both = jnp.concatenate(arrays, axis=along)
    filled, at, gathered = (lax.all_gather(both, axis, axis=dim, tiled=True), 0, [])
    for a in arrays:
        gathered.append(lax.slice_in_dim(filled, at, at + a.shape[along], axis=along))
        at += a.shape[along]
    return tuple(gathered)


def in_blocks(value, dim, size):
    lengths = value.shape
    parts = value.reshape(*lengths[:dim], size, lengths[dim] // size, *lengths[dim + 1 :])
    return jnp.moveaxis(parts, dim, 0)


def summed_on_arrival(value, axis, dim):
    size = lax.axis_size(axis)
    parts = lax.all_to_all(in_blocks(value, dim, size), axis, 0, 0, tiled=True)
    return jnp.sum(parts, axis=0)


def sum_in_two_steps(value, axes, dim):
    far, near = axes
    parts = in_blocks(value, dim, lax.axis_size(far))
    nearer = summed_on_arrival(parts, near, dim + 1)
    arrived = lax.all_to_all(nearer, far, split_axis=0, concat_axis=0, tiled=True)
    return arrived.sum(axis=0)


def padded_to(lines, size):
    spare = -lines.shape[0] % size
    if not spare:
        return lines
    return jnp.concatenate([lines, jnp.zeros((spare, *lines.shape[1:]), lines.dtype)])


def gather_axes(value, axes, dim):
    far, near = axes
    parts = from_everyone(from_everyone(value, far), near)
    return in_order(parts.swapaxes(0, 1).reshape(-1, *value.shape), dim)


def total_of(value, axes):
    own = sum_in_two_steps(
        padded_to(value, lax.axis_size(axes[0]) * lax.axis_size(axes[1])), axes, 0
    )
    whole = gather_axes(own, axes, 0)
    return whole[: len(value)].reshape(value.shape)


def packed_total(arrays, axis):
    vector, at, gathered = (jnp.concatenate([a.reshape(-1) for a in arrays]), 0, [])
    subtotal = total_of(vector, axis)
    for a in arrays:
        gathered.append(subtotal[at : at + a.size].reshape(a.shape))
        at += a.size
    return tuple(gathered)


def gather_in_order(value, axes, sequence):
    parts = value[None]
    for k in sequence:
        parts = lax.all_gather(parts, axes[k], axis=0, tiled=True)
    carried = [lax.axis_size(axes[k]) for k in reversed(sequence)]
    parts = parts.reshape(*carried, *value.shape)
    turned = sorted(range(len(sequence)), key=lambda place: sequence[len(sequence) - 1 - place])
    return parts.transpose(*turned, *range(len(sequence), parts.ndim)).reshape(-1, *value.shape)


def gather_axes_2(value, axes, sequence, dim):
    return in_order(gather_in_order(value, axes, sequence), dim)


def by_axis(value, axes):
    for axis in axes:
        value = lax.psum(value, axis)
    return value


def normalize(values):
    mean = jnp.mean(values, axis=-1, keepdims=True)
    centred = values - mean
    spread = jnp.mean(centred * centred, axis=-1, keepdims=True)
    return centred * lax.rsqrt(spread + EPSILON)


def lookup(table, index):
    onehot = (index[:, None] == jnp.arange(table.shape[0], dtype=jnp.int32)[None, :]).astype(
        jnp.bfloat16
    )
    return jnp.dot(onehot, table, preferred_element_type=jnp.float32)


def slot_update(slots, update, gru_input, gru_hidden):
    width = slots.shape[1]
    from_update = jnp.dot(
        update.astype(jnp.bfloat16), gru_input, preferred_element_type=jnp.float32
    )
    from_state = jnp.dot(slots.astype(jnp.bfloat16), gru_hidden, preferred_element_type=jnp.float32)
    reset = jax.nn.sigmoid(from_update[:, :width] + from_state[:, :width])
    blend = jax.nn.sigmoid(from_update[:, width : 2 * width] + from_state[:, width : 2 * width])
    candidate = jnp.tanh(from_update[:, 2 * width :] + reset * from_state[:, 2 * width :])
    return (1.0 - blend) * candidate + blend * slots


def add_rows(left, piece):
    return jnp.dot(left, piece, preferred_element_type=jnp.float32)


def on_device(
    patches,
    patch_view,
    rays,
    ray_view,
    targets,
    camera,
    slots_init,
    key_weight,
    value_weight,
    query_weight,
    gru_input,
    gru_hidden,
    mix_query,
    mix_key,
    render_in,
    render_out,
):
    width = patches.shape[1]
    scale = width ** (-0.5)
    table = gathered_copies(camera, TOK, 0)
    patch_in = patches.astype(jnp.float32) + lookup(table, patch_view)
    patch_x = normalize(patch_in).astype(jnp.bfloat16)
    pieces = in_one_piece((key_weight, value_weight), TOK, 0, 1)
    keys_sum = add_rows(patch_x, pieces[0])
    values_sum = add_rows(patch_x, pieces[1])
    keys = keys_sum.astype(jnp.bfloat16)
    values = values_sum.astype(jnp.bfloat16)
    query_full, input_full, hidden_full, mixkey_full, colour_full = (
        *in_one_piece((query_weight, gru_input, gru_hidden, mix_key), TOK, 0, 1),
        lax.all_gather(render_out, TOK, axis=1, tiled=True),
    )
    slots = slots_init
    for step in range(ITERS):
        query = (
            jnp.dot(
                normalize(slots).astype(jnp.bfloat16),
                query_full,
                preferred_element_type=jnp.float32,
            )
            * scale
        ).astype(jnp.bfloat16)
        logits = lax.dot_general(
            keys, query, (((1,), (1,)), ((), ())), preferred_element_type=jnp.float32
        )
        attn = jax.nn.softmax(logits, axis=1) + ATTN_FLOOR
        numer = lax.dot_general(
            attn.astype(jnp.bfloat16),
            values,
            (((0,), (0,)), ((), ())),
            preferred_element_type=jnp.float32,
        )
        denom = jnp.sum(attn, axis=0)
        numer, denom = packed_total((numer, denom), (("tok_0", "tok_1"), ("tok_2", "rep")))
        slots = slot_update(slots, numer / denom[:, None], input_full, hidden_full)
    slots_low = slots.astype(jnp.bfloat16)
    ray_in = rays.astype(jnp.float32) + lookup(table, ray_view)
    ray_x = ray_in.astype(jnp.bfloat16)
    ray_rows = ray_x.shape[0]
    query_sum = add_rows(ray_x, gather_axes_2(mix_query, TOK, (1, 0, 2), 0))
    ray_query = (query_sum * scale).astype(jnp.bfloat16)
    slot_keys = jnp.dot(slots_low, mixkey_full, preferred_element_type=jnp.float32).astype(
        jnp.bfloat16
    )
    mix_logits = lax.dot_general(
        ray_query, slot_keys, (((1,), (1,)), ((), ())), preferred_element_type=jnp.float32
    )
    mix = jax.nn.softmax(mix_logits, axis=1).astype(jnp.bfloat16)
    joined = (jnp.dot(mix, slots_low, preferred_element_type=jnp.float32) + ray_in).astype(
        jnp.bfloat16
    )
    pre = add_rows(joined, gather_axes(render_in, (("tok_0", "tok_1"), "tok_2"), 0))
    hidden = jax.nn.silu(pre).astype(jnp.bfloat16)
    colour = lax.dot_general(
        colour_full, hidden, (((1,), (1,)), ((), ())), preferred_element_type=jnp.float32
    )
    error = colour - targets
    rays_total = ray_rows * lax.axis_size(TOK) * lax.axis_size("rep")
    dcol = (error * (2.0 / jnp.sqrt(jnp.float32(3.0 * rays_total)))).astype(jnp.bfloat16)
    squared = jnp.sum(error * error)
    out_part = jnp.dot(dcol, hidden, preferred_element_type=jnp.float32)
    squared, grad_render_out = (by_axis(squared, TOK_REP), by_axis(out_part, TOK_REP))
    loss = squared / (3.0 * rays_total)
    dhidden = lax.dot_general(
        dcol, colour_full, (((0,), (0,)), ((), ())), preferred_element_type=jnp.float32
    )
    sig = jax.nn.sigmoid(pre)
    dpre = (dhidden * (sig + pre * sig * (1.0 - sig))).astype(jnp.bfloat16)
    mine = sum_in_two_steps(
        lax.dot_general(joined, dpre, (((0,), (0,)), ((), ())), preferred_element_type=jnp.float32),
        (("tok_0", "tok_1"), ("tok_2", "rep")),
        0,
    )
    grad_render_in = gathered_copies(mine, "rep", 0)
    return (slots, colour, loss, grad_render_in, grad_render_out)


def solution(mesh):
    torus = Mesh(
        mesh.devices.reshape(8, 4, 2, mesh.shape["rep"]), ("tok_0", "tok_1", "tok_2", "rep")
    )
    return jax.shard_map(
        on_device,
        mesh=torus,
        in_specs=(
            P(TOK_REP, None),
            P(TOK_REP),
            P(TOK_REP, None),
            P(TOK_REP),
            P(None, TOK_REP),
            P(TOK, None),
            P(),
            P(TOK, None),
            P(TOK, None),
            P(TOK, None),
            P(TOK, None),
            P(TOK, None),
            P(TOK, None),
            P(TOK, None),
            P(TOK, None),
            P(None, TOK),
        ),
        out_specs=(P(), P(None, TOK_REP), P(), P(TOK, None), P()),
        check_vma=False,
    )
```

profile of v0, /device:TPU:32, one launch (start us, length us, event | category | flops | bytes accessed | tf_op | source)
XLA Modules:
  0.0 691.2 jit_solution(10916712915491983667)
XLA Ops:
  13.0 11.8 %all-to-all-start = ((bf16[64,8,768]{2,1,0:T(8,128)(2,1)}), bf16[64,8,768]{2,1,0:T(8,128)(2,1)S(1)}, u32[]{:S(2)}, u32[]{:S(2)}) async-start(bf16[64,8,768]{2,1,0:T(8,128)(2,1)} %broadcast_in_dim.28), calls=%async_computation | async-start | bytes 1572864 | tf_op jit(solution)/shard_map/all_to_all | solution.py:16
  25.1 23.2 %all-to-all-done = bf16[64,8,768]{2,1,0:T(8,128)(2,1)S(1)} async-done(((bf16[64,8,768]{2,1,0:T(8,128)(2,1)}), bf16[64,8,768]{2,1,0:T(8,128)(2,1)S(1)}, u32[]{:S(2)}, u32[]{:S(2)}) %all-to-all-start) | async-done | bytes 786464 | tf_op jit(solution)/shard_map/all_to_all | solution.py:16
  49.0 43.4 %all-gather.11.cloned.1.call-done = bf16[64,12,1536]{2,1,0:T(8,128)(2,1)} async-done(((bf16[1,12,1536]{2,1,0:T(8,128)(2,1)}), bf16[64,12,1536]{2,1,0:T(8,128)(2,1)}) %all-gather.11.cloned.1.call-update) | async-done | bytes 2359312 | tf_op jit(solution)/shard_map/all_gather | solution.py:34
  92.4 4.9 reshape.143
  99.8 83.6 %all-gather.13.cloned.1.call-done = bf16[64,12,6144]{2,1,0:T(8,128)(2,1)} async-done(((bf16[1,12,6144]{2,1,0:T(8,128)(2,1)}), bf16[64,12,6144]{2,1,0:T(8,128)(2,1)}) %all-gather.13.cloned.1.call-update) | async-done | bytes 9437200 | tf_op jit(solution)/shard_map/all_gather | solution.py:34
  183.4 13.7 %reshape.145 = bf16[768,6144]{1,0:T(8,128)(2,1)} reshape(bf16[64,12,6144]{2,1,0:T(8,128)(2,1)} %all-gather.13.cloned.1.call-done) | data formatting | bytes 18874368
  199.9 10.9 %all_to_all.105 = f32[8,32,193]{2,1,0:T(8,128)S(1)} all-to-all(f32[8,32,193]{2,1,0:T(8,128)S(1)} %copy.54), channel_id=1, replica_groups=mesh['tok_0'=8,'tok_1'=4,'tok_2'=2,'rep'=4] {'tok_2','rep'}, dimensions={0} | all-to-all | bytes 395264 | tf_op jit(solution)/shard_map/all_to_all | solution.py:49
  210.9 14.4 %all_to_all.106 = f32[32,1,193]{2,1,0:T(1,128)S(1)} all-to-all(f32[32,1,193]{2,1,0:T(1,128)S(1)} %all_to_all.68), channel_id=1, replica_groups=mesh['tok_0'=8,'tok_1'=4,'tok_2'=2,'rep'=4] {'tok_0','tok_1'}, dimensions={0} | all-to-all | bytes 49408 | tf_op jit(solution)/shard_map/all_to_all | solution.py:57
  225.3 12.7 %all_to_all.107 = f32[32,1,193]{2,1,0:T(1,128)S(1)} all-to-all(f32[32,1,193]{2,1,0:T(1,128)S(1)} %broadcast_in_dim.29), channel_id=1, replica_groups=mesh['tok_0'=8,'tok_1'=4,'tok_2'=2,'rep'=4] {'tok_0','tok_1'}, dimensions={0} | all-to-all | bytes 49408 | tf_op jit(solution)/shard_map/all_to_all | solution.py:16
  244.9 4.1 all-to-all-done.4
  255.6 9.7 %all_to_all.108 = f32[8,32,193]{2,1,0:T(8,128)S(1)} all-to-all(f32[8,32,193]{2,1,0:T(8,128)S(1)} %copy.56), channel_id=1, replica_groups=mesh['tok_0'=8,'tok_1'=4,'tok_2'=2,'rep'=4] {'tok_2','rep'}, dimensions={0} | all-to-all | bytes 395264 | tf_op jit(solution)/shard_map/all_to_all | solution.py:49
  265.4 12.8 %all_to_all.109 = f32[32,1,193]{2,1,0:T(1,128)S(1)} all-to-all(f32[32,1,193]{2,1,0:T(1,128)S(1)} %all_to_all.73), channel_id=1, replica_groups=mesh['tok_0'=8,'tok_1'=4,'tok_2'=2,'rep'=4] {'tok_0','tok_1'}, dimensions={0} | all-to-all | bytes 49408 | tf_op jit(solution)/shard_map/all_to_all | solution.py:57
  278.3 12.7 %all_to_all.110 = f32[32,1,193]{2,1,0:T(1,128)S(1)} all-to-all(f32[32,1,193]{2,1,0:T(1,128)S(1)} %broadcast_in_dim.32), channel_id=1, replica_groups=mesh['tok_0'=8,'tok_1'=4,'tok_2'=2,'rep'=4] {'tok_0','tok_1'}, dimensions={0} | all-to-all | bytes 49408 | tf_op jit(solution)/shard_map/all_to_all | solution.py:16
  298.0 3.9 all-to-all-done.8
  308.7 9.9 %all_to_all.111 = f32[8,32,193]{2,1,0:T(8,128)} all-to-all(f32[8,32,193]{2,1,0:T(8,128)S(1)} %copy.58), channel_id=1, replica_groups=mesh['tok_0'=8,'tok_1'=4,'tok_2'=2,'rep'=4] {'tok_2','rep'}, dimensions={0} | all-to-all | bytes 395264 | tf_op jit(solution)/shard_map/all_to_all | solution.py:49
  319.9 5.0 all-to-all-start.13
  325.0 12.6 %all-gather.3 = bf16[4,12,768]{2,1,0:T(8,128)(2,1)S(1)} all-gather(bf16[1,12,768]{2,1,0:T(8,128)(2,1)S(1)} %bitcast.72), channel_id=2, replica_groups=mesh['tok_0'=8,'tok_1'=4,'tok_2'=2,'rep'=4] {'tok_1'}, dimensions={0}, use_global_device_ids=true | all-gather | bytes 92160 | tf_op jit(solution)/shard_map/all_gather | solution.py:94
  337.6 45.5 %all_gather.21 = bf16[32,12,768]{2,1,0:T(8,128)(2,1)S(1)} all-gather(bf16[4,12,768]{2,1,0:T(8,128)(2,1)S(1)} %all-gather.3), channel_id=1, replica_groups=mesh['tok_0'=8,'tok_1'=4,'tok_2'=2,'rep'=4] {'tok_0'}, dimensions={0}, use_global_device_ids=true | all-gather | bytes 663552 | tf_op jit(solution)/shard_map/all_gather | solution.py:94
  385.7 8.1 %all-to-all-start.10 = ((f32[32,1,193]{2,1,0:T(1,128)}), f32[32,1,193]{2,1,0:T(1,128)S(1)}, u32[]{:S(2)}, u32[]{:S(2)}) async-start(f32[32,1,193]{2,1,0:T(1,128)} %all_to_all.78), calls=%async_computation.10 | async-start | bytes 65536 | tf_op jit(solution)/shard_map/all_to_all | solution.py:57
  393.9 43.3 %all-gather.4 = bf16[64,24,3]{1,2,0:T(4,128)(2,1)S(1)} all-gather(bf16[1,24,3]{1,2,0:T(4,128)(2,1)S(1)} %bitcast.73), channel_id=1, replica_groups=mesh['tok_0'=8,'tok_1'=4,'tok_2'=2,'rep'=4] {'tok_0','tok_1','tok_2'}, dimensions={0}, use_global_device_ids=true | all-gather | bytes 9360 | tf_op jit(solution)/shard_map/all_gather | solution.py:171
  451.4 3.9 all-to-all-start.14
  459.1 8.2 %all-to-all-start.11 = ((f32[32,1,193]{2,1,0:T(1,128)}), f32[32,1,193]{2,1,0:T(1,128)S(1)}, u32[]{:S(2)}, u32[]{:S(2)}) async-start(f32[32,1,193]{2,1,0:T(1,128)} %broadcast_in_dim.35), calls=%async_computation.11 | async-start | bytes 65536 | tf_op jit(solution)/shard_map/all_to_all | solution.py:16
  483.2 3.8 all-to-all-done.12
  498.6 5.0 fusion.12
  503.6 7.9 %reshape_reshape.35 = f32[32,8,3,1536]{3,2,1,0:T(4,128)} reshape(f32[768,1536]{1,0:T(8,128)} %fusion.12) | data formatting | bytes 9437184 | tf_op jit(solution)/shard_map/reshape;reshape | solution.py:43
  511.5 5.5 copy.65
  517.0 57.9 %all_to_all.112 = f32[8,32,3,1536]{3,1,2,0:T(8,128)} all-to-all(f32[8,32,3,1536]{3,1,2,0:T(8,128)S(1)} %copy.65), channel_id=1, replica_groups=mesh['tok_0'=8,'tok_1'=4,'tok_2'=2,'rep'=4] {'tok_2','rep'}, dimensions={0} | all-to-all | bytes 9437184 | tf_op jit(solution)/shard_map/all_to_all | solution.py:49
  578.0 30.5 %all_to_all.113 = f32[32,3,1536]{2,1,0:T(4,128)S(1)} all-to-all(f32[32,3,1536]{2,1,0:T(4,128)S(1)} %copy.66), channel_id=1, replica_groups=mesh['tok_0'=8,'tok_1'=4,'tok_2'=2,'rep'=4] {'tok_0','tok_1'}, dimensions={0} | all-to-all | bytes 1179648 | tf_op jit(solution)/shard_map/all_to_all | solution.py:57
  612.8 27.7 %all-reduce = (f32[]{:T(128)}, f32[3,1536]{1,0:T(4,128)S(1)}) all-reduce(f32[]{:T(128)} %get-tuple-element.18, f32[3,1536]{1,0:T(4,128)S(1)} %fusion.145), channel_id=1, replica_groups=mesh['tok_0'=8,'tok_1'=4,'tok_2'=2,'rep'=4] {'tok_0'}, use_global_device_ids=true, to_apply=%region_26.27 | all-reduce | flops 4609 | bytes 36872 | tf_op jit(solution)/shard_map/psum | solution.py:107
  640.6 17.6 %all-reduce.2 = (f32[]{:T(128)}, f32[3,1536]{1,0:T(4,128)S(1)}) all-reduce(f32[]{:T(128)} %get-tuple-element.5, f32[3,1536]{1,0:T(4,128)S(1)} %get-tuple-element.6), channel_id=1, replica_groups=mesh['tok_0'=8,'tok_1'=4,'tok_2'=2,'rep'=4] {'tok_1'}, use_global_device_ids=true, to_apply=%region_27.28 | all-reduce | flops 4609 | bytes 36872 | tf_op jit(solution)/shard_map/psum | solution.py:107
  658.2 4.5 all-reduce.3
  662.7 18.7 %all-reduce.1 = (f32[]{:T(128)}, f32[3,1536]{1,0:T(4,128)}) all-reduce(f32[]{:T(128)} %get-tuple-element.11, f32[3,1536]{1,0:T(4,128)S(1)} %get-tuple-element.12), channel_id=1, replica_groups=mesh['tok_0'=8,'tok_1'=4,'tok_2'=2,'rep'=4] {'rep'}, use_global_device_ids=true, to_apply=%region_29.30 | all-reduce | flops 4609 | bytes 36872 | tf_op jit(solution)/shard_map/psum | solution.py:107
  (154 shorter events, 96.0 us)
Async XLA Ops:
  8.0 16.7 %copy-start.3 = (f32[64,768]{1,0:T(8,128)S(1)}, f32[64,768]{1,0:T(8,128)}, u32[]{:S(2)}) copy-start(f32[64,768]{1,0:T(8,128)} %param.22) | copy-start | bytes 589828
  8.0 40.3 %copy-start.11 = (s32[256]{0:T(256)S(1)}, s32[256]{0:T(256)}, u32[]{:S(2)}) copy-start(s32[256]{0:T(256)} %param.17) | copy-start | bytes 3076
  8.0 40.2 %copy-start.6 = (bf16[256,768]{1,0:T(8,128)(2,1)S(1)}, bf16[256,768]{1,0:T(8,128)(2,1)}, u32[]{:S(2)}) copy-start(bf16[256,768]{1,0:T(8,128)(2,1)} %param.16) | copy-start | bytes 1179652
  8.0 84.4 %all-gather.11.cloned.1.call-start = ((), (), s32[]{:S(2)}) async-start(), calls=%async_computation.19 | async-start | bytes 3194880 | tf_op jit(solution)/shard_map/all_gather | solution.py:34
  9.6 173.8 %all-gather.13.cloned.1.call-start = ((), (), s32[]{:S(2)}) async-start(), calls=%async_computation.20 | async-start | bytes 12779520 | tf_op jit(solution)/shard_map/all_gather | solution.py:34
  13.0 35.3 %all-to-all-start = ((bf16[64,8,768]{2,1,0:T(8,128)(2,1)}), bf16[64,8,768]{2,1,0:T(8,128)(2,1)S(1)}, u32[]{:S(2)}, u32[]{:S(2)}) async-start(bf16[64,8,768]{2,1,0:T(8,128)(2,1)} %broadcast_in_dim.28), calls=%async_computation | async-start | bytes 1572864 | tf_op jit(solution)/shard_map/all_to_all | solution.py:16
  97.3 2.0 copy-start.4
  99.8 153.0 %copy-start.13 = (bf16[256,768]{1,0:T(8,128)(2,1)}, bf16[256,768]{1,0:T(8,128)(2,1)S(1)}, u32[]{:S(2)}) copy-start(bf16[256,768]{1,0:T(8,128)(2,1)S(1)} %convolution_convert_fusion.1) | copy-start | bytes 1179652
  238.8 10.2 %all-to-all-start.4 = ((f32[8,32,193]{2,1,0:T(8,128)}), f32[8,32,193]{2,1,0:T(8,128)S(1)}, u32[]{:S(2)}, u32[]{:S(2)}) async-start(f32[8,32,193]{2,1,0:T(8,128)} %broadcast_in_dim.31), calls=%async_computation.4 | async-start | bytes 524288 | tf_op jit(solution)/shard_map/all_to_all | solution.py:16
  291.7 10.2 %all-to-all-start.8 = ((f32[8,32,193]{2,1,0:T(8,128)}), f32[8,32,193]{2,1,0:T(8,128)S(1)}, u32[]{:S(2)}, u32[]{:S(2)}) async-start(f32[8,32,193]{2,1,0:T(8,128)} %broadcast_in_dim.34), calls=%async_computation.8 | async-start | bytes 524288 | tf_op jit(solution)/shard_map/all_to_all | solution.py:16
  305.8 12.8 %copy-start.7 = (bf16[12,1536]{1,0:T(8,128)(2,1)S(1)}, bf16[12,1536]{1,0:T(8,128)(2,1)}, u32[]{:S(2)}) copy-start(bf16[12,1536]{1,0:T(8,128)(2,1)} %param.30) | copy-start | bytes 110596
  318.6 6.4 copy-start.8
  319.9 65.8 %all-to-all-start.13 = ((bf16[32,12,1536]{2,1,0:T(8,128)(2,1)}), bf16[32,12,1536]{2,1,0:T(8,128)(2,1)S(1)}, u32[]{:S(2)}, u32[]{:S(2)}) async-start(bf16[32,12,1536]{2,1,0:T(8,128)(2,1)} %broadcast_in_dim.39), calls=%async_computation.13 | async-start | bytes 3145728 | tf_op jit(solution)/shard_map/all_to_all | solution.py:16
  324.9 68.9 %copy-start.12 = (bf16[3,24]{1,0:T(4,128)(2,1)S(1)}, bf16[3,24]{1,0:T(4,128)(2,1)}, u32[]{:S(2)}) copy-start(bf16[3,24]{1,0:T(4,128)(2,1)} %param.31) | copy-start | bytes 436
  324.9 112.4 %all-gather.9.cloned.1.call-start = ((), (), s32[]{:S(2)}) async-start(), calls=%async_computation.18 | async-start | bytes 1769472 | tf_op jit(solution)/shard_map/all_gather | solution.py:94
  385.7 62.8 %all-to-all-start.10 = ((f32[32,1,193]{2,1,0:T(1,128)}), f32[32,1,193]{2,1,0:T(1,128)S(1)}, u32[]{:S(2)}, u32[]{:S(2)}) async-start(f32[32,1,193]{2,1,0:T(1,128)} %all_to_all.78), calls=%async_computation.10 | async-start | bytes 65536 | tf_op jit(solution)/shard_map/all_to_all | solution.py:57
  451.4 15.9 %copy-start.10 = (s32[256]{0:T(256)S(1)}, s32[256]{0:T(256)}, u32[]{:S(2)}) copy-start(s32[256]{0:T(256)} %param.19) | copy-start | bytes 3076
  451.4 7.0 %all-to-all-start.14 = ((bf16[2,32,12,1536]{3,1,2,0:T(8,128)(2,1)}), bf16[2,32,12,1536]{3,1,2,0:T(8,128)(2,1)S(1)}, u32[]{:S(2)}, u32[]{:S(2)}) async-start(bf16[2,32,12,1536]{3,1,2,0:T(8,128)(2,1)} %broadcast_in_dim.40), calls=%async_computation.14 | async-start | bytes 4718592 | tf_op jit(solution)/shard_map/all_to_all | solution.py:16
  458.4 11.2 %copy-start = (bf16[2,32,12,1536]{3,1,2,0:T(8,128)(2,1)}, bf16[2,32,12,1536]{3,1,2,0:T(8,128)(2,1)S(1)}, u32[]{:S(2)}) copy-start(bf16[2,32,12,1536]{3,1,2,0:T(8,128)(2,1)S(1)} %all-to-all-done.14) | copy-start | bytes 7077892
  459.1 16.9 %all-to-all-start.11 = ((f32[32,1,193]{2,1,0:T(1,128)}), f32[32,1,193]{2,1,0:T(1,128)S(1)}, u32[]{:S(2)}, u32[]{:S(2)}) async-start(f32[32,1,193]{2,1,0:T(1,128)} %broadcast_in_dim.35), calls=%async_computation.11 | async-start | bytes 65536 | tf_op jit(solution)/shard_map/all_to_all | solution.py:16
  476.8 10.2 %all-to-all-start.12 = ((f32[8,32,193]{2,1,0:T(8,128)}), f32[8,32,193]{2,1,0:T(8,128)S(1)}, u32[]{:S(2)}, u32[]{:S(2)}) async-start(f32[8,32,193]{2,1,0:T(8,128)} %broadcast_in_dim.37), calls=%async_computation.12 | async-start | bytes 524288 | tf_op jit(solution)/shard_map/all_to_all | solution.py:16
  490.4 2.0 copy-start.1
  490.4 2.0 copy-start.2
  490.6 2.8 copy-start.5
  493.4 3.6 copy-start.9
  609.3 72.7 %all-to-all-start.17 = ((f32[4,3,1536]{2,1,0:T(4,128)}), f32[4,3,1536]{2,1,0:T(4,128)S(1)}, u32[]{:S(2)}, u32[]{:S(2)}) async-start(f32[4,3,1536]{2,1,0:T(4,128)} %broadcast_in_dim.41), calls=%async_computation.17 | async-start | bytes 196608 | tf_op jit(solution)/shard_map/all_to_all | solution.py:16
Sparse Core Ops, SparseCore 0:
  12.2 80.1 all-gather.10
  95.7 87.6 all-gather.12
Sparse Core Ops, SparseCore 1:
  384.2 11.9 all-gather.8
where the time goes:
time: 694 us; the launch traced here: 691 us
  blocking collectives  341 us (49%)
  waiting for transfers between devices  166 us (24%)
  local copies, waits for them, and re-layouts  64.1 us (9%)
  starting transfers between devices  51.1 us (7%)
  matrix products  41.2 us (6%)
  between operations  17.9 us (3%)
  other arithmetic  9.31 us (1%)
    all_gather x2, waiting for transfers between devices, in_one_piece(): lax.all_gather(both, axis, axis=dim, tiled=True)  127 us
    all_to_all x4, blocking collectives, summed_on_arrival(): parts = lax.all_to_all(in_blocks(value, dim, size), axis, 0, 0, tiled=True)  88.5 us
    psum x4, blocking collectives, by_axis(): value = lax.psum(value, axis)  68.5 us
    all_gather x2, blocking collectives, gather_in_order(): parts = lax.all_gather(parts, axes[k], axis=0, tiled=True)  58 us
    all_to_all x3, blocking collectives, sum_in_two_steps(): lax.all_to_all(nearer, far, split_axis=0, concat_axis=0, tiled=True)  57.7 us
    all_gather x1, blocking collectives, on_device(): lax.all_gather(render_out, TOK, axis=1, tiled=True)  43.3 us
    all_to_all x8, starting transfers between devices, from_everyone(): lax.all_to_all(jnp.broadcast_to(value[None], (size, *value.shape)), axis,...  42.8 us
    all_to_all x8, waiting for transfers between devices, from_everyone(): lax.all_to_all(jnp.broadcast_to(value[None], (size, *value.shape)), axis,...  39.3 us
  transfers between devices with their start and end apart: 12, of which 8 were waited for; matrix products, arithmetic and copies ran while one was open for 6% of the time, Pallas kernels for 0%

commit v1 on v0

--- a/solution.py
+++ b/solution.py
@@ -168,7 +168,9 @@
     values = values_sum.astype(jnp.bfloat16)
     query_full, input_full, hidden_full, mixkey_full, colour_full = (
         *in_one_piece((query_weight, gru_input, gru_hidden, mix_key), TOK, 0, 1),
-        lax.all_gather(render_out, TOK, axis=1, tiled=True),
+        jnp.concatenate(
+            lax.all_to_all(jnp.stack([render_out] * lax.axis_size(TOK)), TOK, 0, 0), axis=1
+        ),
     )
     slots = slots_init
     for step in range(ITERS):

time: 694 us -> 667 us (0.961)
  blocking collectives: 341 us -> 298 us
  starting transfers between devices: 51.1 us -> 61.4 us
    all_gather x1 -> x0, blocking collectives: 43.3 us -> none  [on_device(): lax.all_gather(render_out, TOK, axis=1, tiled=True)]
    unnamed x34 -> x33, local copies, waits for them, and re-layouts: 18.9 us -> 18.8 us
  transfers between devices with their start and end apart: 12 -> 13, of which waited for: 8 -> 10; matrix products, arithmetic and copies ran while one was open for 6% -> 7% of each run, Pallas kernels for 0% -> 0%
where the time goes in v1:
time: 667 us; the launch traced here: 664 us
  blocking collectives  298 us (45%)
  waiting for transfers between devices  171 us (26%)
  local copies, waits for them, and re-layouts  64.8 us (10%)
  starting transfers between devices  61.4 us (9%)
  matrix products  41.2 us (6%)
  between operations  17.9 us (3%)
  other arithmetic  9.31 us (1%)
    all_gather x2, waiting for transfers between devices, in_one_piece(): lax.all_gather(both, axis, axis=dim, tiled=True)  127 us
    all_to_all x4, blocking collectives, summed_on_arrival(): parts = lax.all_to_all(in_blocks(value, dim, size), axis, 0, 0, tiled=True)  88.5 us
    psum x4, blocking collectives, by_axis(): value = lax.psum(value, axis)  68.5 us
    all_gather x2, blocking collectives, gather_in_order(): parts = lax.all_gather(parts, axes[k], axis=0, tiled=True)  58 us
    all_to_all x3, blocking collectives, sum_in_two_steps(): lax.all_to_all(nearer, far, split_axis=0, concat_axis=0, tiled=True)  57.7 us
    all_to_all x8, starting transfers between devices, from_everyone(): lax.all_to_all(jnp.broadcast_to(value[None], (size, *value.shape)), axis,...  47.9 us
    all_to_all x8, waiting for transfers between devices, from_everyone(): lax.all_to_all(jnp.broadcast_to(value[None], (size, *value.shape)), axis,...  39.7 us
    all_to_all x2, blocking collectives, from_everyone(): lax.all_to_all(jnp.broadcast_to(value[None], (size, *value.shape)), axis,...  25.3 us
  transfers between devices with their start and end apart: 13, of which 10 were waited for; matrix products, arithmetic and copies ran while one was open for 7% of the time, Pallas kernels for 0%

profile of v1, /device:TPU:32, one launch (start us, length us, event | category | flops | bytes accessed | tf_op | source)
XLA Modules:
  0.0 663.7 jit_solution(1991844985618394575)
XLA Ops:
  13.0 11.8 %all-to-all-start = ((bf16[64,8,768]{2,1,0:T(8,128)(2,1)}), bf16[64,8,768]{2,1,0:T(8,128)(2,1)S(1)}, u32[]{:S(2)}, u32[]{:S(2)}) async-start(bf16[64,8,768]{2,1,0:T(8,128)(2,1)} %broadcast_in_dim.28), calls=%async_computation | async-start | bytes 1572864 | tf_op jit(solution)/shard_map/all_to_all | solution.py:16
  25.1 23.2 %all-to-all-done = bf16[64,8,768]{2,1,0:T(8,128)(2,1)S(1)} async-done(((bf16[64,8,768]{2,1,0:T(8,128)(2,1)}), bf16[64,8,768]{2,1,0:T(8,128)(2,1)S(1)}, u32[]{:S(2)}, u32[]{:S(2)}) %all-to-all-start) | async-done | bytes 786464 | tf_op jit(solution)/shard_map/all_to_all | solution.py:16
  49.0 43.4 %all-gather.10.cloned.1.call-done = bf16[64,12,1536]{2,1,0:T(8,128)(2,1)} async-done(((bf16[1,12,1536]{2,1,0:T(8,128)(2,1)}), bf16[64,12,1536]{2,1,0:T(8,128)(2,1)}) %all-gather.10.cloned.1.call-update) | async-done | bytes 2359312 | tf_op jit(solution)/shard_map/all_gather | solution.py:34
  92.4 4.9 reshape.153
  99.8 83.6 %all-gather.12.cloned.1.call-done = bf16[64,12,6144]{2,1,0:T(8,128)(2,1)} async-done(((bf16[1,12,6144]{2,1,0:T(8,128)(2,1)}), bf16[64,12,6144]{2,1,0:T(8,128)(2,1)}) %all-gather.12.cloned.1.call-update) | async-done | bytes 9437200 | tf_op jit(solution)/shard_map/all_gather | solution.py:34
  183.4 13.7 %reshape.155 = bf16[768,6144]{1,0:T(8,128)(2,1)} reshape(bf16[64,12,6144]{2,1,0:T(8,128)(2,1)} %all-gather.12.cloned.1.call-done) | data formatting | bytes 18874368
  199.9 10.9 %all_to_all.110 = f32[8,32,193]{2,1,0:T(8,128)S(1)} all-to-all(f32[8,32,193]{2,1,0:T(8,128)S(1)} %copy.53), channel_id=1, replica_groups=mesh['tok_0'=8,'tok_1'=4,'tok_2'=2,'rep'=4] {'tok_2','rep'}, dimensions={0} | all-to-all | bytes 395264 | tf_op jit(solution)/shard_map/all_to_all | solution.py:49
  210.9 14.4 %all_to_all.111 = f32[32,1,193]{2,1,0:T(1,128)S(1)} all-to-all(f32[32,1,193]{2,1,0:T(1,128)S(1)} %all_to_all.71), channel_id=1, replica_groups=mesh['tok_0'=8,'tok_1'=4,'tok_2'=2,'rep'=4] {'tok_0','tok_1'}, dimensions={0} | all-to-all | bytes 49408 | tf_op jit(solution)/shard_map/all_to_all | solution.py:57
  225.3 12.7 %all_to_all.112 = f32[32,1,193]{2,1,0:T(1,128)S(1)} all-to-all(f32[32,1,193]{2,1,0:T(1,128)S(1)} %broadcast_in_dim.29), channel_id=1, replica_groups=mesh['tok_0'=8,'tok_1'=4,'tok_2'=2,'rep'=4] {'tok_0','tok_1'}, dimensions={0} | all-to-all | bytes 49408 | tf_op jit(solution)/shard_map/all_to_all | solution.py:16
  244.9 4.1 all-to-all-done.4
  255.6 9.7 %all_to_all.113 = f32[8,32,193]{2,1,0:T(8,128)S(1)} all-to-all(f32[8,32,193]{2,1,0:T(8,128)S(1)} %copy.55), channel_id=1, replica_groups=mesh['tok_0'=8,'tok_1'=4,'tok_2'=2,'rep'=4] {'tok_2','rep'}, dimensions={0} | all-to-all | bytes 395264 | tf_op jit(solution)/shard_map/all_to_all | solution.py:49
  265.4 12.8 %all_to_all.114 = f32[32,1,193]{2,1,0:T(1,128)S(1)} all-to-all(f32[32,1,193]{2,1,0:T(1,128)S(1)} %all_to_all.76), channel_id=1, replica_groups=mesh['tok_0'=8,'tok_1'=4,'tok_2'=2,'rep'=4] {'tok_0','tok_1'}, dimensions={0} | all-to-all | bytes 49408 | tf_op jit(solution)/shard_map/all_to_all | solution.py:57
  278.3 12.7 %all_to_all.115 = f32[32,1,193]{2,1,0:T(1,128)S(1)} all-to-all(f32[32,1,193]{2,1,0:T(1,128)S(1)} %broadcast_in_dim.32), channel_id=1, replica_groups=mesh['tok_0'=8,'tok_1'=4,'tok_2'=2,'rep'=4] {'tok_0','tok_1'}, dimensions={0} | all-to-all | bytes 49408 | tf_op jit(solution)/shard_map/all_to_all | solution.py:16
  298.0 4.1 all-to-all-done.8
  302.7 5.4 all-to-all-start.15
  317.3 9.9 %all_to_all.116 = f32[8,32,193]{2,1,0:T(8,128)} all-to-all(f32[8,32,193]{2,1,0:T(8,128)S(1)} %copy.57), channel_id=1, replica_groups=mesh['tok_0'=8,'tok_1'=4,'tok_2'=2,'rep'=4] {'tok_2','rep'}, dimensions={0} | all-to-all | bytes 395264 | tf_op jit(solution)/shard_map/all_to_all | solution.py:49
  328.6 7.6 %all-to-all-start.13 = ((bf16[32,12,1536]{2,1,0:T(8,128)(2,1)}), bf16[32,12,1536]{2,1,0:T(8,128)(2,1)S(1)}, u32[]{:S(2)}, u32[]{:S(2)}) async-start(bf16[32,12,1536]{2,1,0:T(8,128)(2,1)} %broadcast_in_dim.39), calls=%async_computation.13 | async-start | bytes 3145728 | tf_op jit(solution)/shard_map/all_to_all | solution.py:16
  336.2 12.7 %all-gather.3 = bf16[4,12,768]{2,1,0:T(8,128)(2,1)S(1)} all-gather(bf16[1,12,768]{2,1,0:T(8,128)(2,1)S(1)} %bitcast.69), channel_id=2, replica_groups=mesh['tok_0'=8,'tok_1'=4,'tok_2'=2,'rep'=4] {'tok_1'}, dimensions={0}, use_global_device_ids=true | all-gather | bytes 92160 | tf_op jit(solution)/shard_map/all_gather | solution.py:94
  348.9 45.4 %all_gather.18 = bf16[32,12,768]{2,1,0:T(8,128)(2,1)S(1)} all-gather(bf16[4,12,768]{2,1,0:T(8,128)(2,1)S(1)} %all-gather.3), channel_id=1, replica_groups=mesh['tok_0'=8,'tok_1'=4,'tok_2'=2,'rep'=4] {'tok_0'}, dimensions={0}, use_global_device_ids=true | all-gather | bytes 663552 | tf_op jit(solution)/shard_map/all_gather | solution.py:94
  396.9 7.9 %all-to-all-start.10 = ((f32[32,1,193]{2,1,0:T(1,128)}), f32[32,1,193]{2,1,0:T(1,128)S(1)}, u32[]{:S(2)}, u32[]{:S(2)}) async-start(f32[32,1,193]{2,1,0:T(1,128)} %all_to_all.81), calls=%async_computation.10 | async-start | bytes 65536 | tf_op jit(solution)/shard_map/all_to_all | solution.py:57
  428.8 10.1 %all-to-all-start.11 = ((f32[32,1,193]{2,1,0:T(1,128)}), f32[32,1,193]{2,1,0:T(1,128)S(1)}, u32[]{:S(2)}, u32[]{:S(2)}) async-start(f32[32,1,193]{2,1,0:T(1,128)} %broadcast_in_dim.35), calls=%async_computation.11 | async-start | bytes 65536 | tf_op jit(solution)/shard_map/all_to_all | solution.py:16
  448.4 4.3 all-to-all-start.12
  455.4 4.1 all-to-all-done.12
  471.1 5.0 fusion.12
  476.1 7.9 %reshape_reshape.35 = f32[32,8,3,1536]{3,2,1,0:T(4,128)} reshape(f32[768,1536]{1,0:T(8,128)} %fusion.12) | data formatting | bytes 9437184 | tf_op jit(solution)/shard_map/reshape;reshape | solution.py:43
  484.0 5.5 copy.64
  489.5 57.9 %all_to_all.117 = f32[8,32,3,1536]{3,1,2,0:T(8,128)} all-to-all(f32[8,32,3,1536]{3,1,2,0:T(8,128)S(1)} %copy.64), channel_id=1, replica_groups=mesh['tok_0'=8,'tok_1'=4,'tok_2'=2,'rep'=4] {'tok_2','rep'}, dimensions={0} | all-to-all | bytes 9437184 | tf_op jit(solution)/shard_map/all_to_all | solution.py:49
  550.5 30.5 %all_to_all.118 = f32[32,3,1536]{2,1,0:T(4,128)S(1)} all-to-all(f32[32,3,1536]{2,1,0:T(4,128)S(1)} %copy.65), channel_id=1, replica_groups=mesh['tok_0'=8,'tok_1'=4,'tok_2'=2,'rep'=4] {'tok_0','tok_1'}, dimensions={0} | all-to-all | bytes 1179648 | tf_op jit(solution)/shard_map/all_to_all | solution.py:57
  585.3 27.7 %all-reduce = (f32[]{:T(128)}, f32[3,1536]{1,0:T(4,128)S(1)}) all-reduce(f32[]{:T(128)} %get-tuple-element.18, f32[3,1536]{1,0:T(4,128)S(1)} %fusion.145), channel_id=1, replica_groups=mesh['tok_0'=8,'tok_1'=4,'tok_2'=2,'rep'=4] {'tok_0'}, use_global_device_ids=true, to_apply=%region_26.27 | all-reduce | flops 4609 | bytes 36872 | tf_op jit(solution)/shard_map/psum | solution.py:107
  613.1 17.6 %all-reduce.2 = (f32[]{:T(128)}, f32[3,1536]{1,0:T(4,128)S(1)}) all-reduce(f32[]{:T(128)} %get-tuple-element.5, f32[3,1536]{1,0:T(4,128)S(1)} %get-tuple-element.6), channel_id=1, replica_groups=mesh['tok_0'=8,'tok_1'=4,'tok_2'=2,'rep'=4] {'tok_1'}, use_global_device_ids=true, to_apply=%region_27.28 | all-reduce | flops 4609 | bytes 36872 | tf_op jit(solution)/shard_map/psum | solution.py:107
  630.7 4.5 all-reduce.3
  635.2 18.7 %all-reduce.1 = (f32[]{:T(128)}, f32[3,1536]{1,0:T(4,128)}) all-reduce(f32[]{:T(128)} %get-tuple-element.11, f32[3,1536]{1,0:T(4,128)S(1)} %get-tuple-element.12), channel_id=1, replica_groups=mesh['tok_0'=8,'tok_1'=4,'tok_2'=2,'rep'=4] {'rep'}, use_global_device_ids=true, to_apply=%region_29.30 | all-reduce | flops 4609 | bytes 36872 | tf_op jit(solution)/shard_map/psum | solution.py:107
  (156 shorter events, 101.4 us)
Async XLA Ops:
  8.0 16.7 %copy-start.3 = (f32[64,768]{1,0:T(8,128)S(1)}, f32[64,768]{1,0:T(8,128)}, u32[]{:S(2)}) copy-start(f32[64,768]{1,0:T(8,128)} %param.22) | copy-start | bytes 589828
  8.0 40.3 %copy-start.11 = (s32[256]{0:T(256)S(1)}, s32[256]{0:T(256)}, u32[]{:S(2)}) copy-start(s32[256]{0:T(256)} %param.17) | copy-start | bytes 3076
  8.0 40.2 %copy-start.6 = (bf16[256,768]{1,0:T(8,128)(2,1)S(1)}, bf16[256,768]{1,0:T(8,128)(2,1)}, u32[]{:S(2)}) copy-start(bf16[256,768]{1,0:T(8,128)(2,1)} %param.16) | copy-start | bytes 1179652
  8.0 84.4 %all-gather.10.cloned.1.call-start = ((), (), s32[]{:S(2)}) async-start(), calls=%async_computation.20 | async-start | bytes 3194880 | tf_op jit(solution)/shard_map/all_gather | solution.py:34
  9.6 173.8 %all-gather.12.cloned.1.call-start = ((), (), s32[]{:S(2)}) async-start(), calls=%async_computation.21 | async-start | bytes 12779520 | tf_op jit(solution)/shard_map/all_gather | solution.py:34
  13.0 35.3 %all-to-all-start = ((bf16[64,8,768]{2,1,0:T(8,128)(2,1)}), bf16[64,8,768]{2,1,0:T(8,128)(2,1)S(1)}, u32[]{:S(2)}, u32[]{:S(2)}) async-start(bf16[64,8,768]{2,1,0:T(8,128)(2,1)} %broadcast_in_dim.28), calls=%async_computation | async-start | bytes 1572864 | tf_op jit(solution)/shard_map/all_to_all | solution.py:16
  97.3 2.0 copy-start.4
  99.8 153.0 %copy-start.13 = (bf16[256,768]{1,0:T(8,128)(2,1)}, bf16[256,768]{1,0:T(8,128)(2,1)S(1)}, u32[]{:S(2)}) copy-start(bf16[256,768]{1,0:T(8,128)(2,1)S(1)} %convolution_convert_fusion.1) | copy-start | bytes 1179652
  238.8 10.2 %all-to-all-start.4 = ((f32[8,32,193]{2,1,0:T(8,128)}), f32[8,32,193]{2,1,0:T(8,128)S(1)}, u32[]{:S(2)}, u32[]{:S(2)}) async-start(f32[8,32,193]{2,1,0:T(8,128)} %broadcast_in_dim.31), calls=%async_computation.4 | async-start | bytes 524288 | tf_op jit(solution)/shard_map/all_to_all | solution.py:16
  291.7 10.4 %copy-start.12 = (bf16[3,24]{1,0:T(4,128)(2,1)S(1)}, bf16[3,24]{1,0:T(4,128)(2,1)}, u32[]{:S(2)}) copy-start(bf16[3,24]{1,0:T(4,128)(2,1)} %param.31) | copy-start | bytes 436
  291.7 10.4 %all-to-all-start.8 = ((f32[8,32,193]{2,1,0:T(8,128)}), f32[8,32,193]{2,1,0:T(8,128)S(1)}, u32[]{:S(2)}, u32[]{:S(2)}) async-start(f32[8,32,193]{2,1,0:T(8,128)} %broadcast_in_dim.34), calls=%async_computation.8 | async-start | bytes 524288 | tf_op jit(solution)/shard_map/all_to_all | solution.py:16
  302.7 14.6 %all-to-all-start.15 = ((bf16[64,3,24]{2,1,0:T(4,128)(2,1)}), bf16[64,3,24]{2,1,0:T(4,128)(2,1)S(1)}, u32[]{:S(2)}, u32[]{:S(2)}) async-start(bf16[64,3,24]{2,1,0:T(4,128)(2,1)} %stack.2), calls=%async_computation.15 | async-start | bytes 131072 | tf_op jit(solution)/shard_map/all_to_all | solution.py:172
  312.0 15.3 %copy-start.7 = (bf16[12,1536]{1,0:T(8,128)(2,1)S(1)}, bf16[12,1536]{1,0:T(8,128)(2,1)}, u32[]{:S(2)}) copy-start(bf16[12,1536]{1,0:T(8,128)(2,1)} %param.30) | copy-start | bytes 110596
  327.3 9.0 %copy-start.8 = (bf16[12,768]{1,0:T(8,128)(2,1)S(1)}, bf16[12,768]{1,0:T(8,128)(2,1)}, u32[]{:S(2)}) copy-start(bf16[12,768]{1,0:T(8,128)(2,1)} %param.28) | copy-start | bytes 55300
  328.6 68.3 %all-to-all-start.13 = ((bf16[32,12,1536]{2,1,0:T(8,128)(2,1)}), bf16[32,12,1536]{2,1,0:T(8,128)(2,1)S(1)}, u32[]{:S(2)}, u32[]{:S(2)}) async-start(bf16[32,12,1536]{2,1,0:T(8,128)(2,1)} %broadcast_in_dim.39), calls=%async_computation.13 | async-start | bytes 3145728 | tf_op jit(solution)/shard_map/all_to_all | solution.py:16
  336.2 70.9 %all-gather.8.cloned.1.call-start = ((), (), s32[]{:S(2)}) async-start(), calls=%async_computation.19 | async-start | bytes 1769472 | tf_op jit(solution)/shard_map/all_gather | solution.py:94
  396.9 21.3 %all-to-all-start.10 = ((f32[32,1,193]{2,1,0:T(1,128)}), f32[32,1,193]{2,1,0:T(1,128)S(1)}, u32[]{:S(2)}, u32[]{:S(2)}) async-start(f32[32,1,193]{2,1,0:T(1,128)} %all_to_all.81), calls=%async_computation.10 | async-start | bytes 65536 | tf_op jit(solution)/shard_map/all_to_all | solution.py:57
  421.1 17.8 %copy-start.10 = (s32[256]{0:T(256)S(1)}, s32[256]{0:T(256)}, u32[]{:S(2)}) copy-start(s32[256]{0:T(256)} %param.19) | copy-start | bytes 3076
  421.1 7.0 %all-to-all-start.14 = ((bf16[2,32,12,1536]{3,1,2,0:T(8,128)(2,1)}), bf16[2,32,12,1536]{3,1,2,0:T(8,128)(2,1)S(1)}, u32[]{:S(2)}, u32[]{:S(2)}) async-start(bf16[2,32,12,1536]{3,1,2,0:T(8,128)(2,1)} %broadcast_in_dim.40), calls=%async_computation.14 | async-start | bytes 4718592 | tf_op jit(solution)/shard_map/all_to_all | solution.py:16
  428.1 13.1 %copy-start = (bf16[2,32,12,1536]{3,1,2,0:T(8,128)(2,1)}, bf16[2,32,12,1536]{3,1,2,0:T(8,128)(2,1)S(1)}, u32[]{:S(2)}) copy-start(bf16[2,32,12,1536]{3,1,2,0:T(8,128)(2,1)S(1)} %all-to-all-done.14) | copy-start | bytes 7077892
  428.8 18.9 %all-to-all-start.11 = ((f32[32,1,193]{2,1,0:T(1,128)}), f32[32,1,193]{2,1,0:T(1,128)S(1)}, u32[]{:S(2)}, u32[]{:S(2)}) async-start(f32[32,1,193]{2,1,0:T(1,128)} %broadcast_in_dim.35), calls=%async_computation.11 | async-start | bytes 65536 | tf_op jit(solution)/shard_map/all_to_all | solution.py:16
  448.4 11.1 %all-to-all-start.12 = ((f32[8,32,193]{2,1,0:T(8,128)}), f32[8,32,193]{2,1,0:T(8,128)S(1)}, u32[]{:S(2)}, u32[]{:S(2)}) async-start(f32[8,32,193]{2,1,0:T(8,128)} %broadcast_in_dim.37), calls=%async_computation.12 | async-start | bytes 524288 | tf_op jit(solution)/shard_map/all_to_all | solution.py:16
  462.9 2.0 copy-start.1
  462.9 2.0 copy-start.2
  463.1 2.8 copy-start.5
  465.9 3.6 copy-start.9
  581.8 72.7 %all-to-all-start.18 = ((f32[4,3,1536]{2,1,0:T(4,128)}), f32[4,3,1536]{2,1,0:T(4,128)S(1)}, u32[]{:S(2)}, u32[]{:S(2)}) async-start(f32[4,3,1536]{2,1,0:T(4,128)} %broadcast_in_dim.41), calls=%async_computation.18 | async-start | bytes 196608 | tf_op jit(solution)/shard_map/all_to_all | solution.py:16
Sparse Core Ops, SparseCore 0:
  12.2 80.1 all-gather.9
  95.7 87.6 all-gather.11
Sparse Core Ops, SparseCore 1:
  395.4 11.6 all-gather.7
